TPU v7x, 32 devices: a whole 2x2x4 slice. The times are simulated.
32 devices in a mesh: groups: 2 (over y), space: 4 (over z), chan: 2 (over x), rep: 2 (over core).
Axes of the slice: x: 2, y: 2, z: 4, core: 2. Of those that a mesh axis runs over, the one named last changes fastest.
Arguments:
- volume: bfloat16 [4, 8, 32, 8, 128], P(('groups', 'rep'), 'space', 'chan'), parts along dimension 0, may hold values from -6 to 6
- early_weight: bfloat16 [3, 3, 3, 128, 128], replicated, may hold values from -0.109375 to 0.109375
- late_weight: bfloat16 [3, 3, 3, 128, 512], P(None, None, None, None, 'chan'), may hold values from -0.109375 to 0.109375
- cotangent: bfloat16 [4, 4, 16, 4, 512], P(('groups', 'rep'), 'space', None, None, 'chan'), parts along dimension 0, may hold values from -6 to 6
Outputs:
- grad_early: bfloat16 [6, 3, 3, 128, 128], P('groups'), parts along dimension 0
- grad_late: bfloat16 [6, 3, 3, 128, 512], P('groups', None, None, None, 'chan'), parts along dimension 0
- grad_volume: bfloat16 [4, 8, 32, 8, 128], P(('groups', 'rep'), 'space', 'chan'), parts along dimension 0
There are 2 independent parts, one for each index of `groups`. A program takes and returns all parts, laid end to end along the dimension named above; an argument that names none is the same for every part. Nothing has to cross between parts.
All inputs are finite; a program needn't handle non-finite values.
Results may differ from a plain program's by a relative error of at most 0.0065.
Values may be sent and summed in bfloat16 or wider, within the bound.
No kernel may reach another device: no remote copies, remote signals or barrier semaphores. Data moves between devices by JAX's collectives and lax.ppermute only.
A program may use at most 64 MiB of HBM per device.

v0:
```python
import math
import jax
import jax.numpy as jnp
from jax import lax
from jax.sharding import PartitionSpec as P


def padded_2(block, sides, width):
    for axis, dim in sides:
        count = lax.axis_size(axis)
        forward = [(i, i + 1) for i in range(count - 1)]
        backward = [(target, source) for source, target in forward]
        low = lax.ppermute(
            lax.slice_in_dim(block, block.shape[dim] - width, None, axis=dim), axis, forward
        )
        high = lax.ppermute(lax.slice_in_dim(block, 0, width, axis=dim), axis, backward)
        block = jnp.concatenate([low, block, high], axis=dim)
    return block


def gelu_tanh(value):
    return jax.nn.gelu(value, approximate=True)


def conv_padded(padded, weight):
    depth = padded.shape[1] - 2
    height = padded.shape[2] - 2
    length = padded.shape[3] - 2
    total = None
    for first in range(3):
        for second in range(3):
            for third in range(3):
                window = padded[
                    :, first : first + depth, second : second + height, third : third + length
                ]
                term = jnp.einsum(
                    "sxyzc,co->sxyzo",
                    window,
                    weight[first, second, third],
                    preferred_element_type=jnp.float32,
                )
                total = term if total is None else total + term
    return total


def kernel_grad(padded, delta):
    depth = delta.shape[1]
    height = delta.shape[2]
    length = delta.shape[3]
    planes = []
    for first in range(3):
        for second in range(3):
            for third in range(3):
                window = padded[
                    :, first : first + depth, second : second + height, third : third + length
                ]
                planes.append(
                    jnp.einsum("sxyzc,sxyzo->co", window, delta, preferred_element_type=jnp.float32)
                )
    stacked = jnp.stack(planes, axis=0)
    return stacked.reshape((3, 3, 3) + stacked.shape[1:])


def flipped(weight):
    return jnp.swapaxes(weight[::-1, ::-1, ::-1], 3, 4)


def pad_dims(field, dims):
    widths = [(1, 1) if place in dims else (0, 0) for place in range(field.ndim)]
    return jnp.pad(field, widths)


def pool_cells(field):
    s, x, y, z, c = field.shape
    return jnp.mean(field.reshape(s, x // 2, 2, y // 2, 2, z // 2, 2, c), axis=(2, 4, 6))


def spread_cells(field):
    s, x, y, z, c = field.shape
    wide = jnp.broadcast_to(field[:, :, None, :, None, :, None, :], (s, x, 2, y, 2, z, 2, c))
    return wide.reshape(s, 2 * x, 2 * y, 2 * z, c) * 0.125


def late_layer(joined, late_weight, cotangent):
    rim = padded_2(joined, (("space", 1),), 1)
    late_pad = pad_dims(rim, (2, 3))
    pre_late = conv_padded(late_pad, late_weight)
    delta_late = jax.vjp(gelu_tanh, pre_late)[1](cotangent.astype(jnp.float32))[0].astype(
        jnp.bfloat16
    )
    late_part = kernel_grad(late_pad, delta_late)
    delta_rim = padded_2(delta_late, (("space", 1),), 1)
    back_partial = conv_padded(pad_dims(delta_rim, (2, 3)), flipped(late_weight))
    return (back_partial, late_part)


def per_device(volume, early_weight, late_weight, cotangent):
    count = (
        cotangent.shape[0]
        * lax.axis_size("rep")
        * cotangent.shape[1]
        * lax.axis_size("space")
        * cotangent.shape[2]
        * cotangent.shape[3]
    )
    scale = 1.0 / math.sqrt(count)
    haloed = padded_2(volume, (("space", 1), ("chan", 2)), 1)
    padded_in = pad_dims(haloed, (3,))
    pre_early = conv_padded(padded_in, early_weight)
    pooled = pool_cells(gelu_tanh(pre_early)).astype(jnp.bfloat16)
    joined = lax.all_gather(pooled, "chan", axis=2, tiled=True)
    back_partial, late_part = late_layer(joined, late_weight, cotangent)
    back_rows = lax.psum_scatter(back_partial, "chan", scatter_dimension=2, tiled=True)
    delta_early = jax.vjp(gelu_tanh, pre_early)[1](spread_cells(back_rows))[0].astype(jnp.bfloat16)
    early_part = kernel_grad(padded_in, delta_early)
    delta_halo = padded_2(delta_early, (("space", 1), ("chan", 2)), 1)
    grad_volume = conv_padded(pad_dims(delta_halo, (3,)), flipped(early_weight)).astype(
        jnp.bfloat16
    )
    early_total = lax.psum(early_part, ("space", "chan", "rep"))
    grad_early = (early_total * scale).astype(jnp.bfloat16)
    late_total = lax.psum(late_part, ("space", "rep"))
    grad_late = (late_total * scale).astype(jnp.bfloat16)
    return (grad_early, grad_late, grad_volume)


def solution(mesh):
    return jax.shard_map(
        per_device,
        mesh=mesh,
        in_specs=(
            P(("groups", "rep"), "space", "chan", None, None),
            P(),
            P(None, None, None, None, "chan"),
            P(("groups", "rep"), "space", None, None, "chan"),
        ),
        out_specs=(
            P("groups", None, None, None, None),
            P("groups", None, None, None, "chan"),
            P(("groups", "rep"), "space", "chan", None, None),
        ),
        check_vma=False,
    )
```

profile of v0, /device:TPU:0, one launch (start us, length us, event | category | flops | bytes accessed | tf_op | source)
XLA Modules:
  0.0 279.8 jit_solution(17251219886939649005)
XLA Ops:
  7.2 0.8 fusion.308
  8.0 4.9 %collective-permute-start = (bf16[1,1,16,8,128]{4,3,2,1,0:T(8,128)(2,1)S(1)}, bf16[1,1,16,8,128]{4,3,2,1,0:T(8,128)(2,1)S(1)}, u32[]{:S(2)}, u32[]{:S(2)}) collective-permute-start(bf16[1,1,16,8,128]{4,3,2,1,0:T(8,128)(2,1)S(1)} %get-tuple-element.12), channel_id=1, source_target_pairs={{0,4},{4,8},{8,12},{1,5},{5,9},{9,13},{2,6},{6,10},{10,14},{3,7},{... | collective-permute-start | bytes 98312 | tf_op jit(solution)/shard_map/ppermute | solution.py:13
  12.9 1.4 collective-permute-start.1
  14.4 3.8 %copy.129 = bf16[3,3,3,128,256]{3,4,2,1,0:T(8,128)(2,1)} copy(bf16[3,3,3,128,256]{4,3,2,1,0:T(8,128)(2,1)} %param.6) | data formatting | bytes 3538944 | tf_op args[2]
  18.2 0.6 collective-permute-done.1
  18.9 3.4 %collective-permute-start.2 = (bf16[1,4,1,8,128]{4,3,2,1,0:T(8,128)(2,1)S(1)}, bf16[1,4,1,8,128]{4,3,2,1,0:T(8,128)(2,1)S(1)}, u32[]{:S(2)}, u32[]{:S(2)}) collective-permute-start(bf16[1,4,1,8,128]{4,3,2,1,0:T(8,128)(2,1)S(1)} %get-tuple-element.7), channel_id=1, source_target_pairs={{0,2},{1,3},{4,6},{5,7},{8,10},{9,11},{12,14},{13,15},{16,18},{17,... | collective-permute-start | bytes 24584 | tf_op jit(solution)/shard_map/ppermute | solution.py:13
  22.3 1.4 collective-permute-start.3
  23.7 1.6 reverse_bitcast_fusion
  25.3 1.7 copy.133
  27.0 1.0 collective-permute-done.3
  32.5 4.5 %all-gather = bf16[16,4,128]{2,0,1:T(8,128)(2,1)S(1)} all-gather(bf16[8,4,128]{2,0,1:T(8,128)(2,1)S(1)} %fusion.279), channel_id=2, replica_groups=mesh['groups'=2,'space'=4,'chan'=2,'rep'=2] {'chan'}, dimensions={0}, use_global_device_ids=true | all-gather | bytes 24576 | tf_op jit(solution)/shard_map/all_gather | solution.py:111
  37.0 3.9 %collective-permute-start.4 = (bf16[1,1,16,4,128]{4,2,3,1,0:T(8,128)(2,1)S(1)}, bf16[1,1,16,4,128]{4,2,3,1,0:T(8,128)(2,1)S(1)}, u32[]{:S(2)}, u32[]{:S(2)}) collective-permute-start(bf16[1,1,16,4,128]{4,2,3,1,0:T(8,128)(2,1)S(1)} %bitcast.1506), channel_id=1, source_target_pairs={{0,4},{4,8},{8,12},{1,5},{5,9},{9,13},{2,6},{6,10},{10,14},{3,7},{... | collective-permute-start | bytes 49160 | tf_op jit(solution)/shard_map/ppermute | solution.py:13
  41.0 1.3 collective-permute-start.5
  42.3 1.2 reverse_bitcast_fusion.1
  43.5 3.1 %collective-permute-done.5 = bf16[1,1,16,4,128]{4,2,3,1,0:T(8,128)(2,1)S(1)} collective-permute-done((bf16[1,1,16,4,128]{4,2,3,1,0:T(8,128)(2,1)S(1)}, bf16[1,1,16,4,128]{4,2,3,1,0:T(8,128)(2,1)S(1)}, u32[]{:S(2)}, u32[]{:S(2)}) %collective-permute-start.5) | collective-permute-done | bytes 16416 | tf_op jit(solution)/shard_map/ppermute | solution.py:16
  50.5 3.5 %collective-permute-start.6 = (bf16[1,1,16,4,256]{4,2,3,1,0:T(8,128)(2,1)S(1)}, bf16[1,1,16,4,256]{4,2,3,1,0:T(8,128)(2,1)S(1)}, u32[]{:S(2)}, u32[]{:S(2)}) collective-permute-start(bf16[1,1,16,4,256]{4,2,3,1,0:T(8,128)(2,1)S(1)} %fusion.92), channel_id=1, source_target_pairs={{0,4},{4,8},{8,12},{1,5},{5,9},{9,13},{2,6},{6,10},{10,14},{3,7},{... | collective-permute-start | bytes 98312 | tf_op jit(solution)/shard_map/ppermute | solution.py:13
  54.0 1.3 collective-permute-start.7
  60.1 1.8 copy-done.1
  65.6 0.8 fusion.64
  66.5 0.9 fusion.2
  67.3 10.6 %reduce-scatter.2.cloned.1.call-done = f32[1,1,8,4,128]{4,2,3,1,0:T(8,128)} async-done(((f32[1,1,16,4,128]{4,2,3,1,0:T(8,128)}), f32[1,1,8,4,128]{4,2,3,1,0:T(8,128)}) %reduce-scatter.2.cloned.1.call-update) | async-done | bytes 16400 | tf_op jit(solution)/shard_map/reduce_scatter | solution.py:113
  77.9 0.7 multiply_bitcast_fusion.1
  79.1 0.9 fusion.60
  80.0 0.2 fusion.59
  80.4 0.2 fusion.57
  80.7 0.2 fusion.56
  81.8 0.2 fusion.51
  82.0 0.2 fusion.50
  82.7 0.2 fusion.47
  83.4 0.2 fusion.44
  83.8 0.2 fusion.42
  84.0 0.2 fusion.41
  84.5 0.2 fusion.39
  84.7 0.2 fusion.38
  85.6 1.2 copy-done.4
  87.0 3.4 %collective-permute-start.8 = (bf16[1,1,16,8,128]{4,3,2,1,0:T(8,128)(2,1)S(1)}, bf16[1,1,16,8,128]{4,3,2,1,0:T(8,128)(2,1)S(1)}, u32[]{:S(2)}, u32[]{:S(2)}) collective-permute-start(bf16[1,1,16,8,128]{4,3,2,1,0:T(8,128)(2,1)S(1)} %get-tuple-element.9), channel_id=1, source_target_pairs={{0,4},{4,8},{8,12},{1,5},{5,9},{9,13},{2,6},{6,10},{10,14},{3,7},{... | collective-permute-start | bytes 98312 | tf_op jit(solution)/shard_map/ppermute | solution.py:13
  90.4 1.3 collective-permute-start.9
  91.7 0.9 fusion.1
  92.6 3.8 %collective-permute-done.9 = bf16[1,1,16,8,128]{4,3,2,1,0:T(8,128)(2,1)S(1)} collective-permute-done((bf16[1,1,16,8,128]{4,3,2,1,0:T(8,128)(2,1)S(1)}, bf16[1,1,16,8,128]{4,3,2,1,0:T(8,128)(2,1)S(1)}, u32[]{:S(2)}, u32[]{:S(2)}) %collective-permute-start.9) | collective-permute-done | bytes 32800 | tf_op jit(solution)/shard_map/ppermute | solution.py:16
  96.4 2.7 collective-permute-start.10
  99.1 1.3 collective-permute-start.11
  100.4 0.8 fusion
  101.3 3.4 %collective-permute-done.11 = bf16[1,4,1,8,128]{4,3,2,1,0:T(8,128)(2,1)S(1)} collective-permute-done((bf16[1,4,1,8,128]{4,3,2,1,0:T(8,128)(2,1)S(1)}, bf16[1,4,1,8,128]{4,3,2,1,0:T(8,128)(2,1)S(1)}, u32[]{:S(2)}, u32[]{:S(2)}) %collective-permute-start.11) | collective-permute-done | bytes 8224 | tf_op jit(solution)/shard_map/ppermute | solution.py:16
  109.0 0.8 fusion.34
  109.8 74.2 %all-reduce.7.cloned.1.call-done = f32[3,3,3,128,128]{4,3,2,1,0:T(8,128)} async-done(((f32[3,3,3,128,128]{4,3,2,1,0:T(8,128)}), f32[3,3,3,128,128]{4,3,2,1,0:T(8,128)}) %all-reduce.7.cloned.1.call-update) | async-done | bytes 1769488 | tf_op jit(solution)/shard_map/psum | solution.py:120
  184.0 2.6 multiply_convert_fusion.1
  186.6 83.0 %all-reduce.9.cloned.1.call-done = f32[3,3,3,128,256]{4,3,2,1,0:T(8,128)} async-done(((f32[3,3,3,128,256]{4,3,2,1,0:T(8,128)}), f32[3,3,3,128,256]{4,3,2,1,0:T(8,128)}) %all-reduce.9.cloned.1.call-update) | async-done | bytes 3538960 | tf_op jit(solution)/shard_map/psum | solution.py:122
  269.6 3.7 %multiply_convert_fusion = bf16[3,3,3,128,256]{4,3,2,1,0:T(8,128)(2,1)} fusion(f32[3,3,3,128,256]{4,3,2,1,0:T(8,128)} %all-reduce.9.cloned.1.call-done), kind=kLoop, calls=%fused_computation | loop fusion | flops 1769472 | bytes 5308416 | tf_op jit(solution)/shard_map/convert_element_type | solution.py:123
  (207 shorter events, 24.9 us)
Async XLA Ops:
  7.2 70.8 %reduce-scatter.2.cloned.1.call-start = ((), (), s32[]{:S(2)}) async-start(), calls=%async_computation.1 | async-start | bytes 49152 | tf_op jit(solution)/shard_map/reduce_scatter | solution.py:113
  8.0 10.2 %collective-permute-start = (bf16[1,1,16,8,128]{4,3,2,1,0:T(8,128)(2,1)S(1)}, bf16[1,1,16,8,128]{4,3,2,1,0:T(8,128)(2,1)S(1)}, u32[]{:S(2)}, u32[]{:S(2)}) collective-permute-start(bf16[1,1,16,8,128]{4,3,2,1,0:T(8,128)(2,1)S(1)} %get-tuple-element.12), channel_id=1, source_target_pairs={{0,4},{4,8},{8,12},{1,5},{5,9},{9,13},{2,6},{6,10},{10,14},{3,7},{... | collective-permute-start | bytes 98312 | tf_op jit(solution)/shard_map/ppermute | solution.py:13
  12.9 5.3 %copy-start.3 = (bf16[1,2,16,8,128]{4,3,2,1,0:T(8,128)(2,1)S(1)}, bf16[1,2,16,8,128]{4,3,2,1,0:T(8,128)(2,1)}, u32[]{:S(2)}) copy-start(bf16[1,2,16,8,128]{4,3,2,1,0:T(8,128)(2,1)} %param.4) | copy-start | bytes 196612
  12.9 5.9 %collective-permute-start.1 = (bf16[1,1,16,8,128]{4,3,2,1,0:T(8,128)(2,1)S(1)}, bf16[1,1,16,8,128]{4,3,2,1,0:T(8,128)(2,1)S(1)}, u32[]{:S(2)}, u32[]{:S(2)}) collective-permute-start(bf16[1,1,16,8,128]{4,3,2,1,0:T(8,128)(2,1)S(1)} %get-tuple-element.11), channel_id=1, source_target_pairs={{4,0},{8,4},{12,8},{5,1},{9,5},{13,9},{6,2},{10,6},{14,10},{7,3},{... | collective-permute-start | bytes 98312 | tf_op jit(solution)/shard_map/ppermute | solution.py:16
  18.2 11.2 %copy-start.13 = (bf16[1,1,16,8,128]{4,3,2,1,0:T(8,128)(2,1)}, bf16[1,1,16,8,128]{4,3,2,1,0:T(8,128)(2,1)S(1)}, u32[]{:S(2)}) copy-start(bf16[1,1,16,8,128]{4,3,2,1,0:T(8,128)(2,1)S(1)} %collective-permute-done) | copy-start | bytes 98308
  18.9 13.1 %copy-start.11 = (bf16[1,1,16,8,128]{4,3,2,1,0:T(8,128)(2,1)}, bf16[1,1,16,8,128]{4,3,2,1,0:T(8,128)(2,1)S(1)}, u32[]{:S(2)}) copy-start(bf16[1,1,16,8,128]{4,3,2,1,0:T(8,128)(2,1)S(1)} %collective-permute-done.1) | copy-start | bytes 98308
  18.9 8.1 %collective-permute-start.2 = (bf16[1,4,1,8,128]{4,3,2,1,0:T(8,128)(2,1)S(1)}, bf16[1,4,1,8,128]{4,3,2,1,0:T(8,128)(2,1)S(1)}, u32[]{:S(2)}, u32[]{:S(2)}) collective-permute-start(bf16[1,4,1,8,128]{4,3,2,1,0:T(8,128)(2,1)S(1)} %get-tuple-element.7), channel_id=1, source_target_pairs={{0,2},{1,3},{4,6},{5,7},{8,10},{9,11},{12,14},{13,15},{16,18},{17,... | collective-permute-start | bytes 24584 | tf_op jit(solution)/shard_map/ppermute | solution.py:13
  22.3 3.0 %copy-start.2 = (bf16[3,3,3,128,128]{4,3,2,1,0:T(8,128)(2,1)S(1)}, bf16[3,3,3,128,128]{4,3,2,1,0:T(8,128)(2,1)}, u32[]{:S(2)}) copy-start(bf16[3,3,3,128,128]{4,3,2,1,0:T(8,128)(2,1)} %param.5) | copy-start | bytes 2654212
  22.3 5.7 %collective-permute-start.3 = (bf16[1,4,1,8,128]{4,3,2,1,0:T(8,128)(2,1)S(1)}, bf16[1,4,1,8,128]{4,3,2,1,0:T(8,128)(2,1)S(1)}, u32[]{:S(2)}, u32[]{:S(2)}) collective-permute-start(bf16[1,4,1,8,128]{4,3,2,1,0:T(8,128)(2,1)S(1)} %get-tuple-element.8), channel_id=1, source_target_pairs={{2,0},{3,1},{6,4},{7,5},{10,8},{11,9},{14,12},{15,13},{18,16},{19,... | collective-permute-start | bytes 24584 | tf_op jit(solution)/shard_map/ppermute | solution.py:16
  27.0 4.6 %copy-start.9 = (bf16[1,4,1,8,128]{4,3,2,1,0:T(8,128)(2,1)}, bf16[1,4,1,8,128]{4,3,2,1,0:T(8,128)(2,1)S(1)}, u32[]{:S(2)}) copy-start(bf16[1,4,1,8,128]{4,3,2,1,0:T(8,128)(2,1)S(1)} %collective-permute-done.2) | copy-start | bytes 24580
  28.0 4.3 %copy-start.7 = (bf16[1,4,1,8,128]{4,3,2,1,0:T(8,128)(2,1)}, bf16[1,4,1,8,128]{4,3,2,1,0:T(8,128)(2,1)S(1)}, u32[]{:S(2)}) copy-start(bf16[1,4,1,8,128]{4,3,2,1,0:T(8,128)(2,1)S(1)} %collective-permute-done.3) | copy-start | bytes 24580
  32.5 14.1 %copy-start = (bf16[3,3,3,128,256]{4,3,2,1,0:T(8,128)(2,1)S(1)}, bf16[3,3,3,128,256]{4,3,2,1,0:T(8,128)(2,1)}, u32[]{:S(2)}) copy-start(bf16[3,3,3,128,256]{4,3,2,1,0:T(8,128)(2,1)} %param.6) | copy-start | bytes 5308420
  37.0 6.5 %collective-permute-start.4 = (bf16[1,1,16,4,128]{4,2,3,1,0:T(8,128)(2,1)S(1)}, bf16[1,1,16,4,128]{4,2,3,1,0:T(8,128)(2,1)S(1)}, u32[]{:S(2)}, u32[]{:S(2)}) collective-permute-start(bf16[1,1,16,4,128]{4,2,3,1,0:T(8,128)(2,1)S(1)} %bitcast.1506), channel_id=1, source_target_pairs={{0,4},{4,8},{8,12},{1,5},{5,9},{9,13},{2,6},{6,10},{10,14},{3,7},{... | collective-permute-start | bytes 49160 | tf_op jit(solution)/shard_map/ppermute | solution.py:13
  41.0 5.6 %collective-permute-start.5 = (bf16[1,1,16,4,128]{4,2,3,1,0:T(8,128)(2,1)S(1)}, bf16[1,1,16,4,128]{4,2,3,1,0:T(8,128)(2,1)S(1)}, u32[]{:S(2)}, u32[]{:S(2)}) collective-permute-start(bf16[1,1,16,4,128]{4,2,3,1,0:T(8,128)(2,1)S(1)} %bitcast.1507), channel_id=1, source_target_pairs={{4,0},{8,4},{12,8},{5,1},{9,5},{13,9},{6,2},{10,6},{14,10},{7,3},{... | collective-permute-start | bytes 49160 | tf_op jit(solution)/shard_map/ppermute | solution.py:16
  48.0 2.3 copy-start.15
  50.5 9.6 %collective-permute-start.6 = (bf16[1,1,16,4,256]{4,2,3,1,0:T(8,128)(2,1)S(1)}, bf16[1,1,16,4,256]{4,2,3,1,0:T(8,128)(2,1)S(1)}, u32[]{:S(2)}, u32[]{:S(2)}) collective-permute-start(bf16[1,1,16,4,256]{4,2,3,1,0:T(8,128)(2,1)S(1)} %fusion.92), channel_id=1, source_target_pairs={{0,4},{4,8},{8,12},{1,5},{5,9},{9,13},{2,6},{6,10},{10,14},{3,7},{... | collective-permute-start | bytes 98312 | tf_op jit(solution)/shard_map/ppermute | solution.py:13
  54.0 7.9 %collective-permute-start.7 = (bf16[1,1,16,4,256]{4,2,3,1,0:T(8,128)(2,1)S(1)}, bf16[1,1,16,4,256]{4,2,3,1,0:T(8,128)(2,1)S(1)}, u32[]{:S(2)}, u32[]{:S(2)}) collective-permute-start(bf16[1,1,16,4,256]{4,2,3,1,0:T(8,128)(2,1)S(1)} %fusion.92), channel_id=1, source_target_pairs={{4,0},{8,4},{12,8},{5,1},{9,5},{13,9},{6,2},{10,6},{14,10},{7,3},{... | collective-permute-start | bytes 98312 | tf_op jit(solution)/shard_map/ppermute | solution.py:16
  60.1 1.8 copy-start.1
  66.4 117.6 %all-reduce.7.cloned.1.call-start = ((), (), s32[]{:S(2)}) async-start(), calls=%async_computation.2 | async-start | bytes 3538944 | tf_op jit(solution)/shard_map/psum | solution.py:120
  78.8 6.6 %copy-start.5 = (bf16[2,16,8,128]{3,2,1,0:T(8,128)(2,1)}, bf16[2,16,8,128]{3,2,1,0:T(8,128)(2,1)S(1)}, u32[]{:S(2)}) copy-start(bf16[2,16,8,128]{3,2,1,0:T(8,128)(2,1)S(1)} %fusion.84) | copy-start | bytes 196612
  78.8 1.6 copy-start.14
  80.2 0.9 copy-start.8
  80.9 0.9 copy-start.10
  83.6 0.9 copy-start.12
  85.6 1.2 copy-start.4
  86.8 182.8 %all-reduce.9.cloned.1.call-start = ((), (), s32[]{:S(2)}) async-start(), calls=%async_computation.3 | async-start | bytes 7077888 | tf_op jit(solution)/shard_map/psum | solution.py:122
  87.0 5.6 %collective-permute-start.8 = (bf16[1,1,16,8,128]{4,3,2,1,0:T(8,128)(2,1)S(1)}, bf16[1,1,16,8,128]{4,3,2,1,0:T(8,128)(2,1)S(1)}, u32[]{:S(2)}, u32[]{:S(2)}) collective-permute-start(bf16[1,1,16,8,128]{4,3,2,1,0:T(8,128)(2,1)S(1)} %get-tuple-element.9), channel_id=1, source_target_pairs={{0,4},{4,8},{8,12},{1,5},{5,9},{9,13},{2,6},{6,10},{10,14},{3,7},{... | collective-permute-start | bytes 98312 | tf_op jit(solution)/shard_map/ppermute | solution.py:13
  90.4 6.0 %collective-permute-start.9 = (bf16[1,1,16,8,128]{4,3,2,1,0:T(8,128)(2,1)S(1)}, bf16[1,1,16,8,128]{4,3,2,1,0:T(8,128)(2,1)S(1)}, u32[]{:S(2)}, u32[]{:S(2)}) collective-permute-start(bf16[1,1,16,8,128]{4,3,2,1,0:T(8,128)(2,1)S(1)} %get-tuple-element.10), channel_id=1, source_target_pairs={{4,0},{8,4},{12,8},{5,1},{9,5},{13,9},{6,2},{10,6},{14,10},{7,3},{... | collective-permute-start | bytes 98312 | tf_op jit(solution)/shard_map/ppermute | solution.py:16
  96.4 4.9 %collective-permute-start.10 = (bf16[1,4,1,8,128]{4,3,2,1,0:T(8,128)(2,1)S(1)}, bf16[1,4,1,8,128]{4,3,2,1,0:T(8,128)(2,1)S(1)}, u32[]{:S(2)}, u32[]{:S(2)}) collective-permute-start(bf16[1,4,1,8,128]{4,3,2,1,0:T(8,128)(2,1)S(1)} %get-tuple-element.5), channel_id=1, source_target_pairs={{0,2},{1,3},{4,6},{5,7},{8,10},{9,11},{12,14},{13,15},{16,18},{17,... | collective-permute-start | bytes 24584 | tf_op jit(solution)/shard_map/ppermute | solution.py:13
  99.1 5.5 %collective-permute-start.11 = (bf16[1,4,1,8,128]{4,3,2,1,0:T(8,128)(2,1)S(1)}, bf16[1,4,1,8,128]{4,3,2,1,0:T(8,128)(2,1)S(1)}, u32[]{:S(2)}, u32[]{:S(2)}) collective-permute-start(bf16[1,4,1,8,128]{4,3,2,1,0:T(8,128)(2,1)S(1)} %get-tuple-element.6), channel_id=1, source_target_pairs={{2,0},{3,1},{6,4},{7,5},{10,8},{11,9},{14,12},{15,13},{18,16},{19,... | collective-permute-start | bytes 24584 | tf_op jit(solution)/shard_map/ppermute | solution.py:16
  105.5 1.4 copy-start.6
Sparse Core Ops, SparseCore 0:
  66.6 11.3 reduce-scatter.1
  87.0 96.9 all-reduce.6
  186.5 83.0 all-reduce.8
where the time goes:
time: 281 us; the launch traced here: 280 us
  waiting for transfers between devices  180 us (64%)
  matrix products  31.2 us (11%)
  starting transfers between devices  30 us (11%)
  between operations  14.4 us (5%)
  local copies, waits for them, and re-layouts  12.3 us (4%)
  other arithmetic  7.75 us (3%)
  blocking collectives  4.48 us (2%)
    psum x1, waiting for transfers between devices, per_device(): late_total = lax.psum(late_part, ('space', 'rep'))  83 us
    psum x1, waiting for transfers between devices, per_device(): early_total = lax.psum(early_part, ('space', 'chan', 'rep'))  74.2 us
    ppermute x6, starting transfers between devices, padded_2(): lax.ppermute(lax.slice_in_dim(block, block.shape[dim] - width, None, axis...  21.8 us
    dot_general x108, matrix products, conv_padded(): jnp.einsum('sxyzc,co->sxyzo', window, weight[first, second, third], prefe...  17.4 us
    dot_general x54, matrix products, kernel_grad(): jnp.einsum('sxyzc,sxyzo->co', window, delta, preferred_element_type=jnp.f...  13.9 us
    ppermute x6, waiting for transfers between devices, padded_2(): lax.ppermute(lax.slice_in_dim(block, 0, width, axis=dim), axis, backward)  11.9 us
    reduce_scatter x1, waiting for transfers between devices, per_device(): lax.psum_scatter(back_partial, 'chan', scatter_dimension=2, tiled=True)  10.6 us
    unnamed x36, local copies, waits for them, and re-layouts  8.58 us
  transfers between devices with their start and end apart: 15, of which 8 were waited for; matrix products, arithmetic and copies ran while one was open for 8% of the time, Pallas kernels for 0%

commit v1 on v0

--- a/solution.py
+++ b/solution.py
@@ -117,7 +117,7 @@
     grad_volume = conv_padded(pad_dims(delta_halo, (3,)), flipped(early_weight)).astype(
         jnp.bfloat16
     )
-    early_total = lax.psum(early_part, ("space", "chan", "rep"))
+    early_total = jnp.sum(lax.all_gather(early_part, ("space", "chan", "rep")), axis=0)
     grad_early = (early_total * scale).astype(jnp.bfloat16)
     late_total = lax.psum(late_part, ("space", "rep"))
     grad_late = (late_total * scale).astype(jnp.bfloat16)

time: 281 us -> 301 us (1.071)
  waiting for transfers between devices: 180 us -> 193 us
  other arithmetic: 7.75 us -> 16.5 us
  local copies, waits for them, and re-layouts: 12.3 us -> 9.06 us
    psum x1, waiting for transfers between devices: 83 us -> 169 us  [per_device(): late_total = lax.psum(late_part, ('space', 'rep'))]
    psum x1 -> x0, waiting for transfers between devices: 74.2 us -> none  [per_device(): early_total = lax.psum(early_part, ('space', 'chan', 'rep'))]
    reduce_sum x0 -> x1, other arithmetic: none -> 10.2 us  [per_device(): jnp.sum(lax.all_gather(early_part, ('space', 'chan', 'rep')), axis=0)]
    unnamed x36 -> x16, local copies, waits for them, and re-layouts: 8.58 us -> 8.02 us
  transfers between devices with their start and end apart: 15 -> 15, of which waited for: 8 -> 8; matrix products, arithmetic and copies ran while one was open for 8% -> 9% of each run, Pallas kernels for 0% -> 0%
where the time goes in v1:
time: 301 us; the launch traced here: 300 us
  waiting for transfers between devices  193 us (64%)
  starting transfers between devices  31.7 us (11%)
  matrix products  29.3 us (10%)
  other arithmetic  16.5 us (5%)
  between operations  16.1 us (5%)
  local copies, waits for them, and re-layouts  9.06 us (3%)
  blocking collectives  4.35 us (1%)
    psum x1, waiting for transfers between devices, per_device(): late_total = lax.psum(late_part, ('space', 'rep'))  169 us
    ppermute x6, starting transfers between devices, padded_2(): lax.ppermute(lax.slice_in_dim(block, block.shape[dim] - width, None, axis...  23.6 us
    dot_general x108, matrix products, conv_padded(): jnp.einsum('sxyzc,co->sxyzo', window, weight[first, second, third], prefe...  17.4 us
    ppermute x6, waiting for transfers between devices, padded_2(): lax.ppermute(lax.slice_in_dim(block, 0, width, axis=dim), axis, backward)  13.1 us
    dot_general x54, matrix products, kernel_grad(): jnp.einsum('sxyzc,sxyzo->co', window, delta, preferred_element_type=jnp.f...  11.9 us
    reduce_sum x1, other arithmetic, per_device(): jnp.sum(lax.all_gather(early_part, ('space', 'chan', 'rep')), axis=0)  10.2 us
    reduce_scatter x1, waiting for transfers between devices, per_device(): lax.psum_scatter(back_partial, 'chan', scatter_dimension=2, tiled=True)  9.39 us
    unnamed x16, local copies, waits for them, and re-layouts  8.02 us
  transfers between devices with their start and end apart: 15, of which 8 were waited for; matrix products, arithmetic and copies ran while one was open for 9% of the time, Pallas kernels for 0%

profile of v1, /device:TPU:0, one launch (start us, length us, event | category | flops | bytes accessed | tf_op | source)
XLA Modules:
  0.0 300.0 jit_solution(15391181942776073821)
XLA Ops:
  8.0 0.8 fusion.308
  8.8 4.9 %collective-permute-start = (bf16[1,1,16,8,128]{4,3,2,1,0:T(8,128)(2,1)S(1)}, bf16[1,1,16,8,128]{4,3,2,1,0:T(8,128)(2,1)S(1)}, u32[]{:S(2)}, u32[]{:S(2)}) collective-permute-start(bf16[1,1,16,8,128]{4,3,2,1,0:T(8,128)(2,1)S(1)} %get-tuple-element.12), channel_id=1, source_target_pairs={{0,4},{4,8},{8,12},{1,5},{5,9},{9,13},{2,6},{6,10},{10,14},{3,7},{... | collective-permute-start | bytes 98312 | tf_op jit(solution)/shard_map/ppermute | solution.py:13
  13.7 1.3 collective-permute-start.1
  15.0 0.3 collective-permute-done
  15.3 0.9 constant_dynamic-update-slice_fusion.1
  16.2 3.4 %collective-permute-done.1 = bf16[1,1,16,8,128]{4,3,2,1,0:T(8,128)(2,1)S(1)} collective-permute-done((bf16[1,1,16,8,128]{4,3,2,1,0:T(8,128)(2,1)S(1)}, bf16[1,1,16,8,128]{4,3,2,1,0:T(8,128)(2,1)S(1)}, u32[]{:S(2)}, u32[]{:S(2)}) %collective-permute-start.1) | collective-permute-done | bytes 32800 | tf_op jit(solution)/shard_map/ppermute | solution.py:16
  19.6 3.4 %collective-permute-start.2 = (bf16[1,4,1,8,128]{4,3,2,1,0:T(8,128)(2,1)S(1)}, bf16[1,4,1,8,128]{4,3,2,1,0:T(8,128)(2,1)S(1)}, u32[]{:S(2)}, u32[]{:S(2)}) collective-permute-start(bf16[1,4,1,8,128]{4,3,2,1,0:T(8,128)(2,1)S(1)} %get-tuple-element.7), channel_id=1, source_target_pairs={{0,2},{1,3},{4,6},{5,7},{8,10},{9,11},{12,14},{13,15},{16,18},{17,... | collective-permute-start | bytes 24584 | tf_op jit(solution)/shard_map/ppermute | solution.py:13
  23.0 1.4 collective-permute-start.3
  24.4 2.8 copy.135
  27.2 1.5 collective-permute-done.3
  33.2 4.3 %all-gather = bf16[16,4,128]{2,0,1:T(8,128)(2,1)S(1)} all-gather(bf16[8,4,128]{2,0,1:T(8,128)(2,1)S(1)} %fusion.279), channel_id=2, replica_groups=mesh['groups'=2,'space'=4,'chan'=2,'rep'=2] {'chan'}, dimensions={0}, use_global_device_ids=true | all-gather | bytes 24576 | tf_op jit(solution)/shard_map/all_gather | solution.py:111
  37.6 1.4 collective-permute-start.5
  39.0 4.5 %collective-permute-start.4 = (bf16[1,1,16,4,128]{4,2,3,1,0:T(8,128)(2,1)S(1)}, bf16[1,1,16,4,128]{4,2,3,1,0:T(8,128)(2,1)S(1)}, u32[]{:S(2)}, u32[]{:S(2)}) collective-permute-start(bf16[1,1,16,4,128]{4,2,3,1,0:T(8,128)(2,1)S(1)} %bitcast.1507), channel_id=1, source_target_pairs={{0,4},{4,8},{8,12},{1,5},{5,9},{9,13},{2,6},{6,10},{10,14},{3,7},{... | collective-permute-start | bytes 49160 | tf_op jit(solution)/shard_map/ppermute | solution.py:13
  43.7 1.3 collective-permute-done.4
  48.9 1.3 collective-permute-start.7
  50.2 4.8 %collective-permute-start.6 = (bf16[1,1,16,4,256]{4,2,3,1,0:T(8,128)(2,1)S(1)}, bf16[1,1,16,4,256]{4,2,3,1,0:T(8,128)(2,1)S(1)}, u32[]{:S(2)}, u32[]{:S(2)}) collective-permute-start(bf16[1,1,16,4,256]{4,2,3,1,0:T(8,128)(2,1)S(1)} %fusion.92), channel_id=1, source_target_pairs={{0,4},{4,8},{8,12},{1,5},{5,9},{9,13},{2,6},{6,10},{10,14},{3,7},{... | collective-permute-start | bytes 98312 | tf_op jit(solution)/shard_map/ppermute | solution.py:13
  60.2 1.8 copy-done.1
  65.8 0.8 fusion.64
  66.6 0.8 fusion
  67.5 9.4 %reduce-scatter.2.cloned.1.call-done = f32[1,1,8,4,128]{4,2,3,1,0:T(8,128)} async-done(((f32[1,1,16,4,128]{4,2,3,1,0:T(8,128)}), f32[1,1,8,4,128]{4,2,3,1,0:T(8,128)}) %reduce-scatter.2.cloned.1.call-update) | async-done | bytes 16400 | tf_op jit(solution)/shard_map/reduce_scatter | solution.py:113
  76.9 0.7 multiply_bitcast_fusion.1
  78.0 0.2 fusion.60
  78.3 0.2 fusion.59
  78.7 0.2 fusion.57
  78.9 0.2 fusion.56
  79.4 0.2 fusion.54
  79.6 0.2 fusion.53
  80.0 0.2 fusion.51
  80.2 0.2 fusion.50
  81.6 0.2 fusion.44
  82.0 0.2 fusion.42
  82.2 0.2 fusion.41
  82.7 0.2 fusion.39
  82.9 0.2 fusion.38
  83.6 0.2 fusion.35
  83.8 1.2 copy-done.4
  85.2 3.4 %collective-permute-start.8 = (bf16[1,1,16,8,128]{4,3,2,1,0:T(8,128)(2,1)S(1)}, bf16[1,1,16,8,128]{4,3,2,1,0:T(8,128)(2,1)S(1)}, u32[]{:S(2)}, u32[]{:S(2)}) collective-permute-start(bf16[1,1,16,8,128]{4,3,2,1,0:T(8,128)(2,1)S(1)} %get-tuple-element.9), channel_id=1, source_target_pairs={{0,4},{4,8},{8,12},{1,5},{5,9},{9,13},{2,6},{6,10},{10,14},{3,7},{... | collective-permute-start | bytes 98312 | tf_op jit(solution)/shard_map/ppermute | solution.py:13
  88.6 1.3 collective-permute-start.9
  89.9 1.4 copy.139
  91.3 4.0 %collective-permute-done.9 = bf16[1,1,16,8,128]{4,3,2,1,0:T(8,128)(2,1)S(1)} collective-permute-done((bf16[1,1,16,8,128]{4,3,2,1,0:T(8,128)(2,1)S(1)}, bf16[1,1,16,8,128]{4,3,2,1,0:T(8,128)(2,1)S(1)}, u32[]{:S(2)}, u32[]{:S(2)}) %collective-permute-start.9) | collective-permute-done | bytes 32800 | tf_op jit(solution)/shard_map/ppermute | solution.py:16
  95.3 2.5 collective-permute-start.10
  97.8 1.3 collective-permute-start.11
  99.1 4.3 %collective-permute-done.11 = bf16[1,4,1,8,128]{4,3,2,1,0:T(8,128)(2,1)S(1)} collective-permute-done((bf16[1,4,1,8,128]{4,3,2,1,0:T(8,128)(2,1)S(1)}, bf16[1,4,1,8,128]{4,3,2,1,0:T(8,128)(2,1)S(1)}, u32[]{:S(2)}, u32[]{:S(2)}) %collective-permute-start.11) | collective-permute-done | bytes 8224 | tf_op jit(solution)/shard_map/ppermute | solution.py:16
  107.8 0.8 fusion.34
  108.6 168.9 %all-reduce.6.cloned.1.call-done = f32[3,3,3,128,256]{4,3,2,1,0:T(8,128)} async-done(((f32[3,3,3,128,256]{4,3,2,1,0:T(8,128)}), f32[3,3,3,128,256]{4,3,2,1,0:T(8,128)}) %all-reduce.6.cloned.1.call-update) | async-done | bytes 3538960 | tf_op jit(solution)/shard_map/psum | solution.py:122
  277.5 3.7 %multiply_convert_fusion = bf16[3,3,3,128,256]{4,3,2,1,0:T(8,128)(2,1)} fusion(f32[3,3,3,128,256]{4,3,2,1,0:T(8,128)} %all-reduce.6.cloned.1.call-done), kind=kLoop, calls=%fused_computation | loop fusion | flops 1769472 | bytes 5308416 | tf_op jit(solution)/shard_map/convert_element_type | solution.py:123
  281.2 10.2 %reduce_sum.28 = f32[3,3,3,128,128]{4,3,2,1,0:T(8,128)S(1)} reduce(f32[16,3,3,3,128,128]{5,4,3,2,1,0:T(8,128)} %all-gather.3.cloned.1.call-done, f32[]{:T(128)} %constant.5.clone.1), dimensions={0}, to_apply=%region_3.4 | reduce | flops 6635520 | bytes 30081028 | tf_op jit(solution)/shard_map/reduce_sum | solution.py:120
  291.4 1.2 multiply_convert_fusion.1
  (188 shorter events, 25.1 us)
Async XLA Ops:
  8.0 68.9 %reduce-scatter.2.cloned.1.call-start = ((), (), s32[]{:S(2)}) async-start(), calls=%async_computation.1 | async-start | bytes 49152 | tf_op jit(solution)/shard_map/reduce_scatter | solution.py:113
  8.8 6.5 %collective-permute-start = (bf16[1,1,16,8,128]{4,3,2,1,0:T(8,128)(2,1)S(1)}, bf16[1,1,16,8,128]{4,3,2,1,0:T(8,128)(2,1)S(1)}, u32[]{:S(2)}, u32[]{:S(2)}) collective-permute-start(bf16[1,1,16,8,128]{4,3,2,1,0:T(8,128)(2,1)S(1)} %get-tuple-element.12), channel_id=1, source_target_pairs={{0,4},{4,8},{8,12},{1,5},{5,9},{9,13},{2,6},{6,10},{10,14},{3,7},{... | collective-permute-start | bytes 98312 | tf_op jit(solution)/shard_map/ppermute | solution.py:13
  13.7 5.8 %collective-permute-start.1 = (bf16[1,1,16,8,128]{4,3,2,1,0:T(8,128)(2,1)S(1)}, bf16[1,1,16,8,128]{4,3,2,1,0:T(8,128)(2,1)S(1)}, u32[]{:S(2)}, u32[]{:S(2)}) collective-permute-start(bf16[1,1,16,8,128]{4,3,2,1,0:T(8,128)(2,1)S(1)} %get-tuple-element.11), channel_id=1, source_target_pairs={{4,0},{8,4},{12,8},{5,1},{9,5},{13,9},{6,2},{10,6},{14,10},{7,3},{... | collective-permute-start | bytes 98312 | tf_op jit(solution)/shard_map/ppermute | solution.py:16
  19.6 7.6 %collective-permute-start.2 = (bf16[1,4,1,8,128]{4,3,2,1,0:T(8,128)(2,1)S(1)}, bf16[1,4,1,8,128]{4,3,2,1,0:T(8,128)(2,1)S(1)}, u32[]{:S(2)}, u32[]{:S(2)}) collective-permute-start(bf16[1,4,1,8,128]{4,3,2,1,0:T(8,128)(2,1)S(1)} %get-tuple-element.7), channel_id=1, source_target_pairs={{0,2},{1,3},{4,6},{5,7},{8,10},{9,11},{12,14},{13,15},{16,18},{17,... | collective-permute-start | bytes 24584 | tf_op jit(solution)/shard_map/ppermute | solution.py:13
  23.0 5.8 %copy-start.2 = (bf16[3,3,3,128,128]{4,3,2,1,0:T(8,128)(2,1)S(1)}, bf16[3,3,3,128,128]{4,3,2,1,0:T(8,128)(2,1)}, u32[]{:S(2)}) copy-start(bf16[3,3,3,128,128]{4,3,2,1,0:T(8,128)(2,1)} %param.5) | copy-start | bytes 2654212
  23.0 5.7 %collective-permute-start.3 = (bf16[1,4,1,8,128]{4,3,2,1,0:T(8,128)(2,1)S(1)}, bf16[1,4,1,8,128]{4,3,2,1,0:T(8,128)(2,1)S(1)}, u32[]{:S(2)}, u32[]{:S(2)}) collective-permute-start(bf16[1,4,1,8,128]{4,3,2,1,0:T(8,128)(2,1)S(1)} %get-tuple-element.8), channel_id=1, source_target_pairs={{2,0},{3,1},{6,4},{7,5},{10,8},{11,9},{14,12},{15,13},{18,16},{19,... | collective-permute-start | bytes 24584 | tf_op jit(solution)/shard_map/ppermute | solution.py:16
  27.2 2.9 copy-start.3
  37.6 7.4 %copy-start = (bf16[3,3,3,128,256]{4,3,2,1,0:T(8,128)(2,1)S(1)}, bf16[3,3,3,128,256]{4,3,2,1,0:T(8,128)(2,1)}, u32[]{:S(2)}) copy-start(bf16[3,3,3,128,256]{4,3,2,1,0:T(8,128)(2,1)} %param.6) | copy-start | bytes 5308420
  37.6 6.1 %collective-permute-start.5 = (bf16[1,1,16,4,128]{4,2,3,1,0:T(8,128)(2,1)S(1)}, bf16[1,1,16,4,128]{4,2,3,1,0:T(8,128)(2,1)S(1)}, u32[]{:S(2)}, u32[]{:S(2)}) collective-permute-start(bf16[1,1,16,4,128]{4,2,3,1,0:T(8,128)(2,1)S(1)} %bitcast.1506), channel_id=1, source_target_pairs={{4,0},{8,4},{12,8},{5,1},{9,5},{13,9},{6,2},{10,6},{14,10},{7,3},{... | collective-permute-start | bytes 49160 | tf_op jit(solution)/shard_map/ppermute | solution.py:16
  39.0 6.0 %collective-permute-start.4 = (bf16[1,1,16,4,128]{4,2,3,1,0:T(8,128)(2,1)S(1)}, bf16[1,1,16,4,128]{4,2,3,1,0:T(8,128)(2,1)S(1)}, u32[]{:S(2)}, u32[]{:S(2)}) collective-permute-start(bf16[1,1,16,4,128]{4,2,3,1,0:T(8,128)(2,1)S(1)} %bitcast.1507), channel_id=1, source_target_pairs={{0,4},{4,8},{8,12},{1,5},{5,9},{9,13},{2,6},{6,10},{10,14},{3,7},{... | collective-permute-start | bytes 49160 | tf_op jit(solution)/shard_map/ppermute | solution.py:13
  46.4 2.3 copy-start.5
  48.9 11.4 %collective-permute-start.7 = (bf16[1,1,16,4,256]{4,2,3,1,0:T(8,128)(2,1)S(1)}, bf16[1,1,16,4,256]{4,2,3,1,0:T(8,128)(2,1)S(1)}, u32[]{:S(2)}, u32[]{:S(2)}) collective-permute-start(bf16[1,1,16,4,256]{4,2,3,1,0:T(8,128)(2,1)S(1)} %fusion.92), channel_id=1, source_target_pairs={{4,0},{8,4},{12,8},{5,1},{9,5},{13,9},{6,2},{10,6},{14,10},{7,3},{... | collective-permute-start | bytes 98312 | tf_op jit(solution)/shard_map/ppermute | solution.py:16
  50.2 11.9 %collective-permute-start.6 = (bf16[1,1,16,4,256]{4,2,3,1,0:T(8,128)(2,1)S(1)}, bf16[1,1,16,4,256]{4,2,3,1,0:T(8,128)(2,1)S(1)}, u32[]{:S(2)}, u32[]{:S(2)}) collective-permute-start(bf16[1,1,16,4,256]{4,2,3,1,0:T(8,128)(2,1)S(1)} %fusion.92), channel_id=1, source_target_pairs={{0,4},{4,8},{8,12},{1,5},{5,9},{9,13},{2,6},{6,10},{10,14},{3,7},{... | collective-permute-start | bytes 98312 | tf_op jit(solution)/shard_map/ppermute | solution.py:13
  60.2 1.8 copy-start.1
  66.5 210.9 %all-reduce.6.cloned.1.call-start = ((), (), s32[]{:S(2)}) async-start(), calls=%async_computation.3 | async-start | bytes 7077888 | tf_op jit(solution)/shard_map/psum | solution.py:122
  67.5 213.7 %all-gather.3.cloned.1.call-start = ((), (), s32[]{:S(2)}) async-start(), calls=%async_computation.2 | async-start | bytes 30081024 | tf_op jit(solution)/shard_map/all_gather | solution.py:120
  83.8 1.2 copy-start.4
  85.2 6.1 %collective-permute-start.8 = (bf16[1,1,16,8,128]{4,3,2,1,0:T(8,128)(2,1)S(1)}, bf16[1,1,16,8,128]{4,3,2,1,0:T(8,128)(2,1)S(1)}, u32[]{:S(2)}, u32[]{:S(2)}) collective-permute-start(bf16[1,1,16,8,128]{4,3,2,1,0:T(8,128)(2,1)S(1)} %get-tuple-element.9), channel_id=1, source_target_pairs={{0,4},{4,8},{8,12},{1,5},{5,9},{9,13},{2,6},{6,10},{10,14},{3,7},{... | collective-permute-start | bytes 98312 | tf_op jit(solution)/shard_map/ppermute | solution.py:13
  88.6 6.7 %collective-permute-start.9 = (bf16[1,1,16,8,128]{4,3,2,1,0:T(8,128)(2,1)S(1)}, bf16[1,1,16,8,128]{4,3,2,1,0:T(8,128)(2,1)S(1)}, u32[]{:S(2)}, u32[]{:S(2)}) collective-permute-start(bf16[1,1,16,8,128]{4,3,2,1,0:T(8,128)(2,1)S(1)} %get-tuple-element.10), channel_id=1, source_target_pairs={{4,0},{8,4},{12,8},{5,1},{9,5},{13,9},{6,2},{10,6},{14,10},{7,3},{... | collective-permute-start | bytes 98312 | tf_op jit(solution)/shard_map/ppermute | solution.py:16
  95.3 3.9 %collective-permute-start.10 = (bf16[1,4,1,8,128]{4,3,2,1,0:T(8,128)(2,1)S(1)}, bf16[1,4,1,8,128]{4,3,2,1,0:T(8,128)(2,1)S(1)}, u32[]{:S(2)}, u32[]{:S(2)}) collective-permute-start(bf16[1,4,1,8,128]{4,3,2,1,0:T(8,128)(2,1)S(1)} %get-tuple-element.5), channel_id=1, source_target_pairs={{0,2},{1,3},{4,6},{5,7},{8,10},{9,11},{12,14},{13,15},{16,18},{17,... | collective-permute-start | bytes 24584 | tf_op jit(solution)/shard_map/ppermute | solution.py:13
  97.8 5.7 %collective-permute-start.11 = (bf16[1,4,1,8,128]{4,3,2,1,0:T(8,128)(2,1)S(1)}, bf16[1,4,1,8,128]{4,3,2,1,0:T(8,128)(2,1)S(1)}, u32[]{:S(2)}, u32[]{:S(2)}) collective-permute-start(bf16[1,4,1,8,128]{4,3,2,1,0:T(8,128)(2,1)S(1)} %get-tuple-element.6), channel_id=1, source_target_pairs={{2,0},{3,1},{6,4},{7,5},{10,8},{11,9},{14,12},{15,13},{18,16},{19,... | collective-permute-start | bytes 24584 | tf_op jit(solution)/shard_map/ppermute | solution.py:16
Sparse Core Ops, SparseCore 0:
  66.7 10.1 reduce-scatter.1
  85.2 170.5 all-gather.2
Sparse Core Ops, SparseCore 1:
  69.4 208.0 all-reduce.5
